TPU v7x, 32 devices: a whole 2x2x4 slice. The times are simulated.
32 devices in a mesh: segment: 4 (over z), seq: 4 (over y, core), dp: 2 (over x).
Axes of the slice: x: 2, y: 2, z: 4, core: 2. Of those that a mesh axis runs over, the one named last changes fastest.
Arguments:
- clean: bfloat16 [2, 512, 64], P('dp', 'seq'), may hold values from -16 to 16
- noise: bfloat16 [2, 512, 128], P('dp', 'seq'), may hold values from -24 to 24
- timesteps: int32 [2, 2], replicated, may hold values from 20 to 979
- text_vec: float32 [2, 256], P('dp'), may hold values from -6 to 6
- w_embed: bfloat16 [4, 64, 3072], P('segment'), may hold values from -0.75 to 0.75
- w_time: bfloat16 [4, 256, 3072], P('segment'), may hold values from -0.375 to 0.375
- w_mod: bfloat16 [4, 3072, 15360], P('segment', None, 'seq'), may hold values from -0.109375 to 0.109375
- w_qkv: bfloat16 [4, 3072, 4, 3, 128], P('segment', None, 'seq'), may hold values from -0.109375 to 0.109375
- w_out: bfloat16 [4, 4, 128, 3072], P('segment', 'seq'), may hold values from -0.25 to 0.25
- qk_gain: float32 [4, 2, 128], P('segment'), may hold values from 1.5 to 2.5
- w_final: bfloat16 [4, 3072, 64], P('segment'), may hold values from -0.109375 to 0.109375
Outputs:
- sample_grad: float32 [2, 512, 64], P('dp', 'seq')
- final_grads: float32 [4, 3072, 64], P('segment')
All inputs are finite; a program needn't handle non-finite values. Where the computation divides by a largest or mean magnitude, that divisor is 1e-20 or more.
Results may differ from a plain program's by a relative error of at most 0.025.
Values may be sent and summed in bfloat16 or wider, within the bound.
No kernel may reach another device: no remote copies, remote signals or barrier semaphores. Data moves between devices by JAX's collectives and lax.ppermute only.
A program may use at most 192 MiB of HBM per device.

v0:
```python
import math
import jax
import jax.numpy as jnp
from jax import lax
from jax.sharding import PartitionSpec as P

SHIFT = 7.0
EPS = 1e-06
ADV_WEIGHT = 3.0


def from_root(value, axis, source):
    kept = jnp.where(lax.axis_index(axis) == source, value, 0).astype(value.dtype)
    return lax.psum(kept, axis)


def noise_level(step):
    fraction = step.astype(jnp.float32) / 1000.0
    return SHIFT * fraction / (1.0 + (SHIFT - 1.0) * fraction)


def time_features(step, feature_count):
    half_width = feature_count // 2
    frequency = jnp.exp(-math.log(10000.0) * jnp.arange(half_width, dtype=jnp.float32) / half_width)
    angles = step.astype(jnp.float32) * frequency
    return jnp.concatenate([jnp.cos(angles), jnp.sin(angles)])


def condition(step, text_row, time_w, mod_w):
    features = (time_features(step, text_row.shape[0]) + text_row).astype(jnp.bfloat16)
    hidden = jax.nn.silu(jnp.dot(features, time_w, preferred_element_type=jnp.float32)).astype(
        jnp.bfloat16
    )
    return jnp.dot(hidden, mod_w, preferred_element_type=jnp.float32)


def normalize(values):
    row_mean = jnp.mean(values, axis=-1, keepdims=True)
    centered = values - row_mean
    inverse = lax.rsqrt(jnp.mean(centered * centered, axis=-1, keepdims=True) + EPS)
    return (centered * inverse, inverse)


def normalize_back(gradient, normed, inverse):
    return inverse * (
        gradient
        - jnp.mean(gradient, axis=-1, keepdims=True)
        - normed * jnp.mean(gradient * normed, axis=-1, keepdims=True)
    )


def rms_scale(values, gain_vec):
    inverse = lax.rsqrt(jnp.mean(values * values, axis=-1, keepdims=True) + EPS)
    unit_vec = values * inverse
    return (unit_vec * gain_vec, unit_vec, inverse)


def rms_back(gradient, unit_vec, inverse, gain_vec):
    scaled = gradient * gain_vec
    return inverse * (scaled - unit_vec * jnp.mean(scaled * unit_vec, axis=-1, keepdims=True))


def head_front(normed_in, head_w, gains):
    head_width = head_w.shape[-1]
    flat_w = head_w.reshape(head_w.shape[0], 3 * head_width)
    projected = jnp.dot(normed_in, flat_w, preferred_element_type=jnp.float32)
    queries, q_unit, q_inverse = rms_scale(projected[:, :head_width], gains[0])
    key_vecs, k_unit, k_inverse = rms_scale(projected[:, head_width : 2 * head_width], gains[1])
    query_b = queries.astype(jnp.bfloat16)
    key_b = key_vecs.astype(jnp.bfloat16)
    value_b = projected[:, 2 * head_width :].astype(jnp.bfloat16)
    scores = jnp.dot(query_b, key_b.T, preferred_element_type=jnp.float32) / math.sqrt(head_width)
    weights = jnp.exp(scores)
    soft_max = weights / jnp.sum(weights, axis=-1, keepdims=True)
    head_out = jnp.dot(
        soft_max.astype(jnp.bfloat16), value_b, preferred_element_type=jnp.float32
    ).astype(jnp.bfloat16)
    return (head_out, (q_unit, q_inverse, k_unit, k_inverse, query_b, key_b, value_b, soft_max))


def head_back(grad_out, stored, gains):
    q_unit, q_inverse, k_unit, k_inverse, query_b, key_b, value_b, soft_max = stored
    head_width = query_b.shape[-1]
    grad_soft = jnp.dot(grad_out, value_b.T, preferred_element_type=jnp.float32)
    grad_value = jnp.dot(
        soft_max.astype(jnp.bfloat16).T, grad_out, preferred_element_type=jnp.float32
    )
    grad_scores = soft_max * (grad_soft - jnp.sum(soft_max * grad_soft, axis=-1, keepdims=True))
    grad_scores_b = (grad_scores / math.sqrt(head_width)).astype(jnp.bfloat16)
    grad_query = jnp.dot(grad_scores_b, key_b, preferred_element_type=jnp.float32)
    grad_key = jnp.dot(grad_scores_b.T, query_b, preferred_element_type=jnp.float32)
    grad_q = rms_back(grad_query, q_unit, q_inverse, gains[0])
    grad_k = rms_back(grad_key, k_unit, k_inverse, gains[1])
    return jnp.concatenate([grad_q, grad_k, grad_value], axis=1).astype(jnp.bfloat16)


def guarded(active, func, operand):
    return lax.cond(active, func, lambda item: jax.tree.map(jnp.zeros_like, func(item)), operand)


def shards(
    clean, noise, timesteps, text_vec, w_embed, w_time, w_mod, w_qkv, w_out, qk_gain, w_final
):
    section = lax.axis_index("segment")
    batch_idx = lax.axis_index("dp")
    tok_rows = clean.shape[1]
    latent_width = clean.shape[2]
    model_width = w_embed.shape[2]
    seq_devices = lax.axis_size("seq")
    full_rows = tok_rows * seq_devices
    head_width = w_qkv.shape[4]
    head_total = w_qkv.shape[2] * seq_devices
    group_count = max(
        [
            count
            for count in range(1, seq_devices + 1)
            if seq_devices % count == 0 and count * tok_rows <= max(512, tok_rows)
        ]
    )
    block_rows = group_count * tok_rows
    block_total = full_rows // block_rows
    embed_w = w_embed[0]
    embed_f32 = embed_w.astype(jnp.float32)
    head_w = w_qkv[0, :, 0]
    flat_head_w = head_w.reshape(model_width, 3 * head_width)
    gains = qk_gain[0]
    final_w = w_final[0]
    step_pair = lax.dynamic_index_in_dim(timesteps, batch_idx, 0, keepdims=False)
    sigma_student = noise_level(step_pair[0])
    sigma_critic = noise_level(step_pair[1])
    own_step = jnp.where(section == 0, step_pair[0], step_pair[1])
    mod_piece = condition(own_step, text_vec[0], w_time[0], w_mod[0])
    modulation = lax.all_gather(mod_piece, "seq", axis=0, tiled=True)
    shift_in, scale_in, gate_vec, shift_out, scale_out = [
        modulation[slot * model_width : (slot + 1) * model_width] for slot in range(5)
    ]
    gathered_rows = lax.all_gather(w_out[0], "seq", axis=0, tiled=True)

    def input_rows(latent_block):
        embedded = jnp.dot(latent_block, embed_w, preferred_element_type=jnp.float32)
        normed, inverse = normalize(embedded)
        return (normed, inverse)

    def modulated_rows(latent_block):
        normed, _ = input_rows(latent_block)
        return (normed * (1.0 + scale_in) + shift_in).astype(jnp.bfloat16)

    def forward(latent_local, active):
        latent_all = lax.all_gather(latent_local, "seq", axis=0, tiled=True)

        def front(latent_rows):
            blocks = latent_rows.reshape(block_total, block_rows, latent_width)
            normed_in = lax.map(modulated_rows, blocks).reshape(full_rows, model_width)
            return head_front(normed_in, head_w, gains)

        head_out, stored = guarded(active, front, latent_all)
        own_rows = jnp.dot(latent_local, embed_w, preferred_element_type=jnp.float32)
        local_heads = lax.all_to_all(head_out, "seq", split_axis=0, concat_axis=1, tiled=True)

        def project(mixed):
            stacked = mixed.reshape(tok_rows, head_total, head_width)
            per_head = jnp.einsum(
                "thk,hkd->htd", stacked, gathered_rows, preferred_element_type=jnp.float32
            )
            return jnp.sum(
                lax.optimization_barrier(per_head.astype(jnp.bfloat16)).astype(jnp.float32), axis=0
            )

        attended = guarded(active, project, local_heads)
        residual = own_rows + gate_vec * attended
        normed_out, inverse_out = normalize(residual)
        final_in = (normed_out * (1.0 + scale_out) + shift_out).astype(jnp.bfloat16)
        result = jnp.dot(final_in, final_w, preferred_element_type=jnp.float32)
        return (result, final_in, (latent_all, stored, normed_out, inverse_out))

    noisy_student = (
        (1.0 - sigma_student) * clean[0].astype(jnp.float32)
        + sigma_student * noise[0, :, :latent_width].astype(jnp.float32)
    ).astype(jnp.bfloat16)
    velocity, student_in, _ = forward(noisy_student, section == 0)
    sample = noisy_student.astype(jnp.float32) - sigma_student * velocity
    sample = from_root(sample.astype(jnp.bfloat16), "segment", 0).astype(sample.dtype)
    second_noise = noise[0, :, latent_width:].astype(jnp.float32)
    noisy_critic = ((1.0 - sigma_critic) * sample + sigma_critic * second_noise).astype(
        jnp.bfloat16
    )
    critic_out, critic_in, cache = forward(noisy_critic, section >= 1)
    latent_all, stored, normed_out, inverse_out = cache
    is_judge = section == 3
    grad_logit = -jax.nn.sigmoid(-critic_out)
    grad_final = jnp.dot(
        grad_logit.astype(jnp.bfloat16), final_w.T, preferred_element_type=jnp.float32
    )
    grad_residual = normalize_back(grad_final * (1.0 + scale_out), normed_out, inverse_out)
    grad_attended = (gate_vec * grad_residual).astype(jnp.bfloat16)

    def spread_heads(grad_rows):
        per_head = jnp.einsum(
            "td,hkd->thk", grad_rows, gathered_rows, preferred_element_type=jnp.float32
        )
        return per_head.astype(jnp.bfloat16).reshape(tok_rows, head_total * head_width)

    grad_local = guarded(is_judge, spread_heads, grad_attended)
    grad_head = lax.all_to_all(grad_local, "seq", split_axis=1, concat_axis=0, tiled=True)
    grad_proj = guarded(is_judge, lambda grad_in: head_back(grad_in, stored, gains), grad_head)

    def latent_rows(first_row, row_count):

        def through(pieces):
            proj_rows, latent_block = pieces
            normed_rows, inverse_rows = input_rows(latent_block)
            grad_normed = jnp.dot(proj_rows, flat_head_w.T, preferred_element_type=jnp.float32)
            grad_embedded = normalize_back(
                grad_normed * (1.0 + scale_in), normed_rows, inverse_rows
            )
            return jnp.dot(grad_embedded, embed_f32.T, precision=lax.Precision.HIGHEST)

        pieces = tuple((source for source in (grad_proj, latent_all)))
        return guarded(is_judge, through, pieces)

    grad_latent = lax.psum_scatter(
        latent_rows(jnp.int32(0), tok_rows * lax.axis_size("seq")).astype(jnp.bfloat16),
        "seq",
        scatter_dimension=0,
        tiled=True,
    ).astype(jnp.float32)
    grad_latent = grad_latent + jnp.dot(grad_residual, embed_f32.T, precision=lax.Precision.HIGHEST)
    adverse = (1.0 - sigma_critic) * grad_latent
    real_part = jnp.where(section == 1, sigma_critic * critic_out, 0.0)
    fake_part = jnp.where(section == 2, sigma_critic * critic_out, 0.0)
    judge_part = jnp.where(is_judge, adverse, 0.0)
    real_term, fake_term, adverse_term = (
        lax.psum(real_part.astype(jnp.bfloat16), "segment").astype(jnp.float32),
        lax.psum(fake_part.astype(jnp.bfloat16), "segment").astype(jnp.float32),
        lax.psum(judge_part.astype(jnp.bfloat16), "segment").astype(jnp.float32),
    )
    error_local = jnp.sum(jnp.abs(sample - noisy_critic.astype(jnp.float32) + real_term))
    error_total = lax.psum(error_local, "seq")
    spread = error_total / (full_rows * latent_width) + EPS
    sample_grad = (real_term - fake_term) / spread + ADV_WEIGHT * adverse_term
    target = jnp.where(
        section == 0,
        -sigma_student * sample_grad,
        jnp.where(
            section == 2,
            2.0 * (critic_out - (second_noise - sample)),
            jnp.where(is_judge, jax.nn.sigmoid(critic_out), 0.0),
        ),
    )
    final_rows = jnp.where(section == 0, student_in, critic_in)
    term = jnp.einsum(
        "td,tc->dc", final_rows, target.astype(jnp.bfloat16), preferred_element_type=jnp.float32
    )
    total = lax.psum(term.astype(jnp.bfloat16), ("seq", "dp")).astype(jnp.float32)
    final_grads = total / full_rows
    return (sample_grad[None], final_grads[None])


def solution(mesh):
    placed = (
        P("dp", "seq", None),
        P("dp", "seq", None),
        P(),
        P("dp", None),
        P("segment", None, None),
        P("segment", None, None),
        P("segment", None, "seq"),
        P("segment", None, "seq", None, None),
        P("segment", "seq", None, None),
        P("segment", None, None),
        P("segment", None, None),
    )
    return jax.shard_map(
        shards,
        mesh=mesh,
        in_specs=placed,
        out_specs=(P("dp", "seq", None), P("segment", None, None)),
        check_vma=False,
    )
```

profile of v0, /device:TPU:0, one launch (start us, length us, event | category | flops | bytes accessed | tf_op | source)
XLA Modules:
  0.0 274.7 jit_solution(8759388569653749423)
XLA Ops:
  7.2 0.7 all-gather.5.cloned.1.call-update
  7.9 0.7 constant_dynamic-slice_fusion
  8.6 0.6 fusion.98
  11.1 1.0 fusion.37
  12.2 0.9 fusion.97
  13.2 10.6 %fusion.34 = f32[1,1,3840]{2,1,0:T(1,128)S(1)} fusion(bf16[3072,1]{0,1:T(2,128)(2,1)S(1)} %reshape.223, bf16[1,3072,3840]{2,1,0:T(8,128)(2,1)} %param.31), kind=kOutput, calls=%fused_computation.97 | convolution fusion | flops 23592960 | bytes 23614464 | tf_op jit(solution)/shard_map/dot_general | solution.py:34
  23.8 6.7 %all-gather.2 = f32[4,1,3840]{2,1,0:T(1,128)S(1)} all-gather(f32[1,1,3840]{2,1,0:T(1,128)S(1)} %fusion.34), channel_id=1, replica_groups=mesh['segment'=4,'seq'=4,'dp'=2] {'seq'}, dimensions={0}, use_global_device_ids=true | all-gather | bytes 76800 | tf_op jit(solution)/shard_map/all_gather | solution.py:133
  30.4 6.0 %all-gather = bf16[1,512,64]{1,2,0:T(8,128)(2,1)S(1)} all-gather(bf16[1,128,64]{1,2,0:T(8,128)(2,1)S(1)} %add_convert_fusion.6), channel_id=2, replica_groups=mesh['segment'=4,'seq'=4,'dp'=2] {'seq'}, dimensions={1}, use_global_device_ids=true | all-gather | bytes 81920 | tf_op jit(solution)/shard_map/all_gather | solution.py:149
  36.4 0.6 fusion.96
  37.1 9.9 %conditional.7 = (bf16[512,128]{1,0:T(8,128)(2,1)}) conditional(s32[]{:T(128)} %convert_element_type.187, () %tuple.57, (bf16[512,64]{0,1:T(8,128)(2,1)S(1)}, bf16[64,3072]{1,0:T(8,128)(2,1)S(1)}, f32[3072]{0:T(1024)}, f32[3072]{0:T(1024)}, bf16[1,3072,1,3,128]{4,1,3,2,0:T(8,128)(2,1)S(1)}, /*index=5*/f32[2,128]{1,0:T(2,128)S(1)}) %tuple.157), branch_computations={%region_0.1_spmd, %region_1.7_spmd} | conditional | flops 1559433216 | bytes 40133668 | solution.py:98
  37.1 0.7 broadcast_add_fusion
  37.8 2.4 copy.53
  40.2 1.1 fusion.91
  41.3 0.8 multiply_reduce_fusion
  42.1 0.9 copy-done.13
  43.0 2.4 fusion
  46.0 1.0 convolution_convert_fusion
  47.0 3.3 %all-to-all-start = ((bf16[4,128,128]{2,1,0:T(8,128)(2,1)}), bf16[4,128,128]{2,1,0:T(8,128)(2,1)S(1)}, u32[]{:S(2)}, u32[]{:S(2)}) async-start(bf16[4,128,128]{2,1,0:T(8,128)(2,1)} %bitcast.26), calls=%async_computation | async-start | bytes 262144 | tf_op jit(solution)/shard_map/all_to_all | solution.py:158
  51.0 3.9 %all-to-all-done = bf16[4,128,128]{2,1,0:T(8,128)(2,1)S(1)} async-done(((bf16[4,128,128]{2,1,0:T(8,128)(2,1)}), bf16[4,128,128]{2,1,0:T(8,128)(2,1)S(1)}, u32[]{:S(2)}, u32[]{:S(2)}) %all-to-all-start) | async-done | bytes 131104 | tf_op jit(solution)/shard_map/all_to_all | solution.py:158
  54.9 3.4 %conditional.8 = (f32[128,3072]{1,0:T(8,128)S(1)}) conditional(s32[]{:T(128)} %convert_element_type.187, () %tuple.56, (bf16[128,4,128]{2,0,1:T(8,128)(2,1)S(1)}, bf16[4,128,3072]{2,1,0:T(8,128)(2,1)}) %tuple.152), branch_computations={%region_7.8_spmd, %region_8.10_spmd} | conditional | flops 406978560 | bytes 11141128 | solution.py:98
  54.9 2.9 %convolution_convert_fusion.1 = bf16[4,128,3072]{2,1,0:T(8,128)(2,1)S(1)} fusion(bf16[128,4,128]{2,0,1:T(8,128)(2,1)S(1)} %get-tuple-element.132, bf16[4,128,3072]{2,1,0:T(8,128)(2,1)} %get-tuple-element.133), kind=kOutput, calls=%fused_computation.28 | convolution fusion | flops 404226048 | bytes 6422528 | tf_op jit(solution)/shard_map/cond/branch_1_fun/thk,hkd->htd/dot_general | solution.py:162
  57.7 0.6 convert_reduce_fusion
  58.3 0.5 fusion.99
  59.5 0.9 copy-done.7
  60.8 15.5 %psum.42 = bf16[128,64]{0,1:T(8,128)(2,1)S(1)} all-reduce(bf16[128,64]{0,1:T(8,128)(2,1)S(1)} %fusion.44), channel_id=1, replica_groups=mesh['segment'=4,'seq'=4,'dp'=2] {'segment'}, use_global_device_ids=true, to_apply=%region_12.13 | all-reduce | flops 8192 | bytes 32768 | tf_op jit(solution)/shard_map/psum | solution.py:14
  76.4 5.7 %all_gather.15 = bf16[512,64]{0,1:T(8,128)(2,1)} all-gather(bf16[128,64]{0,1:T(8,128)(2,1)S(1)} %fusion.56), channel_id=1, replica_groups=mesh['segment'=4,'seq'=4,'dp'=2] {'seq'}, dimensions={0}, use_global_device_ids=true | all-gather | bytes 81920 | tf_op jit(solution)/shard_map/all_gather | solution.py:149
  82.1 5.8 %conditional.9 = (bf16[512,128]{1,0:T(8,128)(2,1)S(1)}, f32[512,128]{0,1:T(8,128)}, f32[512,1]{0,1:T(1,128)}, f32[512,128]{0,1:T(8,128)}, f32[512,1]{0,1:T(1,128...) conditional(s32[]{:T(128)} %convert_element_type.194, () %tuple.61, ...), branch_computations={%region_13.14_spmd, %region_14.20_spmd} | conditional | flops 1559433216 | bytes 43594936 | solution.py:98
  82.1 0.6 broadcast.304.clone
  82.7 0.6 broadcast.304
  83.3 0.7 broadcast.302.clone2.1
  83.9 0.7 broadcast.302.clone2
  84.6 0.7 broadcast.302.clone
  85.3 0.7 broadcast.303.clone
  86.0 0.8 broadcast.303
  86.8 1.1 broadcast.305
  87.9 0.7 copy-done.15
  88.5 3.9 %all-to-all-start.1 = ((bf16[4,128,128]{2,1,0:T(8,128)(2,1)}), bf16[4,128,128]{2,1,0:T(8,128)(2,1)}, u32[]{:S(2)}, u32[]{:S(2)}) async-start(bf16[4,128,128]{2,1,0:T(8,128)(2,1)} %bitcast.134), calls=%async_computation.1 | async-start | bytes 262144 | tf_op jit(solution)/shard_map/all_to_all | solution.py:158
  92.5 4.7 %all-to-all-done.1 = bf16[4,128,128]{2,1,0:T(8,128)(2,1)} async-done(((bf16[4,128,128]{2,1,0:T(8,128)(2,1)}), bf16[4,128,128]{2,1,0:T(8,128)(2,1)}, u32[]{:S(2)}, u32[]{:S(2)}) %all-to-all-start.1) | async-done | bytes 131104 | tf_op jit(solution)/shard_map/all_to_all | solution.py:158
  97.2 1.3 conditional.10
  97.2 1.3 broadcast.311
  98.5 1.9 fusion.100
  100.8 1.2 add_convert_fusion.4
  102.0 2.1 select_convert_fusion
  104.1 0.7 fusion.90
  104.8 2.0 multiply_convert_fusion.9
  106.8 0.7 conditional.11
  106.8 0.7 broadcast.312
  107.5 3.3 %all-to-all-start.2 = ((bf16[128,4,128]{0,2,1:T(8,128)(2,1)}), bf16[128,4,128]{0,2,1:T(8,128)(2,1)S(1)}, u32[]{:S(2)}, u32[]{:S(2)}) async-start(bf16[128,4,128]{0,2,1:T(8,128)(2,1)} %bitcast.33), calls=%async_computation.2 | async-start | bytes 262144 | tf_op jit(solution)/shard_map/all_to_all | solution.py:204
  110.9 4.5 %all-to-all-done.2 = bf16[128,4,128]{0,2,1:T(8,128)(2,1)S(1)} async-done(((bf16[128,4,128]{0,2,1:T(8,128)(2,1)}), bf16[128,4,128]{0,2,1:T(8,128)(2,1)S(1)}, u32[]{:S(2)}, u32[]{:S(2)}) %all-to-all-start.2) | async-done | bytes 131104 | tf_op jit(solution)/shard_map/all_to_all | solution.py:204
  115.4 0.7 copy-done.11
  116.2 1.0 copy-done.4
  117.2 0.6 conditional.13
  117.2 0.6 broadcast.316
  117.8 1.7 copy.71
  119.6 60.8 %reduce-scatter.4.cloned.1.call-done = bf16[128,64]{1,0:T(8,128)(2,1)} async-done(((bf16[512,64]{1,0:T(8,128)(2,1)}), bf16[128,64]{1,0:T(8,128)(2,1)}) %reduce-scatter.4.cloned.1.call-update) | async-done | bytes 16400
  180.4 0.8 copy.72
  181.2 2.5 fusion.43
  183.7 19.9 %all-reduce = (bf16[128,64]{0,1:T(8,128)(2,1)S(1)}, bf16[128,64]{0,1:T(8,128)(2,1)S(1)}, bf16[128,64]{0,1:T(8,128)(2,1)S(1)}) all-reduce(bf16[128,64]{0,1:T(8,128)(2,1)S(1)} %fusion.43, bf16[128,64]{0,1:T(8,128)(2,1)} %get-tuple-element.343, ...), channel_id=1, replica_groups=mesh['segment'=4,'seq'=4,'dp'=2] {'segment'}, use_global_device_ids=true, to_apply=%region_45.46 | all-reduce | flops 24576 | bytes 98304 | tf_op jit(solution)/shard_map/psum | solution.py:235
  203.6 1.3 fusion.54
  205.0 6.6 %psum.45 = f32[]{:T(128)} all-reduce(f32[]{:T(128)} %fusion.54), channel_id=1, replica_groups=mesh['segment'=4,'seq'=4,'dp'=2] {'seq'}, use_global_device_ids=true, to_apply=%region_28.29 | all-reduce | flops 1 | bytes 8 | tf_op jit(solution)/shard_map/psum | solution.py:238
  212.1 1.9 convolution_convert_fusion.6
  214.0 0.6 fusion.89
  214.6 51.6 %all-reduce.3.cloned.1.call-done = bf16[3072,64]{0,1:T(8,128)(2,1)} async-done(((bf16[3072,64]{0,1:T(8,128)(2,1)}), bf16[3072,64]{0,1:T(8,128)(2,1)}) %all-reduce.3.cloned.1.call-update) | async-done | bytes 393232 | tf_op jit(solution)/shard_map/psum | solution.py:254
  266.2 1.9 multiply_bitcast_fusion
  (75 shorter events, 2.5 us)
Async XLA Ops:
  7.2 3.9 %copy-start = (bf16[1,256,3072]{2,1,0:T(8,128)(2,1)S(1)}, bf16[1,256,3072]{2,1,0:T(8,128)(2,1)}, u32[]{:S(2)}) copy-start(bf16[1,256,3072]{2,1,0:T(8,128)(2,1)} %param.30) | copy-start | bytes 4718596
  7.2 47.7 %all-gather.5.cloned.1.call-start = ((), (), s32[]{:S(2)}) async-start(), calls=%async_computation.5 | async-start | bytes 3932160 | tf_op jit(solution)/shard_map/all_gather | solution.py:137
  13.2 17.3 %copy-start.26 = (bf16[1,128,64]{1,2,0:T(8,128)(2,1)S(1)}, bf16[1,128,64]{1,2,0:T(8,128)(2,1)}, u32[]{:S(2)}) copy-start(bf16[1,128,64]{1,2,0:T(8,128)(2,1)} %param.25) | copy-start | bytes 49156
  13.2 23.9 %copy-start.3 = (bf16[1,3072,1,3,128]{4,1,3,2,0:T(8,128)(2,1)S(1)}, bf16[1,3072,1,3,128]{4,1,3,2,0:T(8,128)(2,1)}, u32[]{:S(2)}) copy-start(bf16[1,3072,1,3,128]{4,1,3,2,0:T(8,128)(2,1)} %param.32) | copy-start | bytes 7077892
  13.2 23.9 %copy-start.5 = (bf16[1,64,3072]{2,1,0:T(8,128)(2,1)S(1)}, bf16[1,64,3072]{2,1,0:T(8,128)(2,1)}, u32[]{:S(2)}) copy-start(bf16[1,64,3072]{2,1,0:T(8,128)(2,1)} %param.29) | copy-start | bytes 1179652
  13.2 23.9 %copy-start.28 = (f32[1,2,128]{2,1,0:T(2,128)S(1)}, f32[1,2,128]{2,1,0:T(2,128)}, u32[]{:S(2)}) copy-start(f32[1,2,128]{2,1,0:T(2,128)} %param.34) | copy-start | bytes 3076
  37.0 21.3 %copy-start.18 = (f32[3072]{0:T(1024)}, f32[3072]{0:T(1024)S(1)}, u32[]{:S(2)}) copy-start(f32[3072]{0:T(1024)S(1)} %get-tuple-element.341) | copy-start | bytes 36868
  37.0 22.1 %copy-start.20 = (f32[3072]{0:T(1024)}, f32[3072]{0:T(1024)S(1)}, u32[]{:S(2)}) copy-start(f32[3072]{0:T(1024)S(1)} %get-tuple-element.338) | copy-start | bytes 36868
  37.0 22.1 %copy-start.24 = (f32[3072]{0:T(1024)}, f32[3072]{0:T(1024)S(1)}, u32[]{:S(2)}) copy-start(f32[3072]{0:T(1024)S(1)} %get-tuple-element.337) | copy-start | bytes 36868
  41.3 1.7 copy-start.13
  47.0 7.9 %all-to-all-start = ((bf16[4,128,128]{2,1,0:T(8,128)(2,1)}), bf16[4,128,128]{2,1,0:T(8,128)(2,1)S(1)}, u32[]{:S(2)}, u32[]{:S(2)}) async-start(bf16[4,128,128]{2,1,0:T(8,128)(2,1)} %bitcast.26), calls=%async_computation | async-start | bytes 262144 | tf_op jit(solution)/shard_map/all_to_all | solution.py:158
  51.0 25.4 %copy-start.23 = (bf16[1,128,64]{1,2,0:T(8,128)(2,1)}, bf16[1,128,64]{1,2,0:T(8,128)(2,1)S(1)}, u32[]{:S(2)}) copy-start(bf16[1,128,64]{1,2,0:T(8,128)(2,1)S(1)} %copy.74) | copy-start | bytes 49156
  58.3 2.1 copy-start.9
  59.5 0.9 copy-start.7
  76.4 5.7 %copy-start.17 = (bf16[128,64]{0,1:T(8,128)(2,1)}, bf16[128,64]{0,1:T(8,128)(2,1)S(1)}, u32[]{:S(2)}) copy-start(bf16[128,64]{0,1:T(8,128)(2,1)S(1)} %psum.42) | copy-start | bytes 49156
  82.1 15.0 %copy-start.2 = (bf16[4,1,128,3072]{3,2,1,0:T(8,128)(2,1)S(1)}, bf16[4,1,128,3072]{3,2,1,0:T(8,128)(2,1)}, u32[]{:S(2)}) copy-start(bf16[4,1,128,3072]{3,2,1,0:T(8,128)(2,1)} %all-gather.5.cloned.1.call-done) | copy-start | bytes 9437188
  87.9 0.7 copy-start.15
  88.5 8.6 %all-to-all-start.1 = ((bf16[4,128,128]{2,1,0:T(8,128)(2,1)}), bf16[4,128,128]{2,1,0:T(8,128)(2,1)}, u32[]{:S(2)}, u32[]{:S(2)}) async-start(bf16[4,128,128]{2,1,0:T(8,128)(2,1)} %bitcast.134), calls=%async_computation.1 | async-start | bytes 262144 | tf_op jit(solution)/shard_map/all_to_all | solution.py:158
  98.5 2.3 copy-start.21
  98.5 2.3 copy-start.25
  98.5 3.5 %copy-start.10 = (bf16[1,3072,64]{1,2,0:T(8,128)(2,1)S(1)}, bf16[1,3072,64]{1,2,0:T(8,128)(2,1)}, u32[]{:S(2)}) copy-start(bf16[1,3072,64]{1,2,0:T(8,128)(2,1)} %param.35) | copy-start | bytes 1179652
  100.8 4.0 %copy-start.19 = (f32[3072]{0:T(1024)S(1)}, f32[3072]{0:T(1024)}, u32[]{:S(2)}) copy-start(f32[3072]{0:T(1024)} %copy-done.18) | copy-start | bytes 36868
  104.1 0.7 copy-start.16
  107.5 7.9 %all-to-all-start.2 = ((bf16[128,4,128]{0,2,1:T(8,128)(2,1)}), bf16[128,4,128]{0,2,1:T(8,128)(2,1)S(1)}, u32[]{:S(2)}, u32[]{:S(2)}) async-start(bf16[128,4,128]{0,2,1:T(8,128)(2,1)} %bitcast.33), calls=%async_computation.2 | async-start | bytes 262144 | tf_op jit(solution)/shard_map/all_to_all | solution.py:204
  110.8 69.6 %reduce-scatter.4.cloned.1.call-start = ((), (), s32[]{:S(2)}) async-start(), calls=%async_computation.6 | async-start | bytes 163840
  115.4 1.8 copy-start.4
  115.4 0.7 copy-start.11
  117.2 94.9 %copy-start.8 = (bf16[128,3072]{1,0:T(8,128)(2,1)S(1)}, bf16[128,3072]{1,0:T(8,128)(2,1)}, u32[]{:S(2)}) copy-start(bf16[128,3072]{1,0:T(8,128)(2,1)} %copy-done.7) | copy-start | bytes 2359300
  117.8 150.3 %copy-start.1 = (bf16[1,256,3072]{2,1,0:T(8,128)(2,1)S(1)}, bf16[1,256,3072]{2,1,0:T(8,128)(2,1)}, u32[]{:S(2)}) copy-start(bf16[1,256,3072]{2,1,0:T(8,128)(2,1)} %param.30) | copy-start | bytes 4718596
  119.6 146.6 %all-reduce.3.cloned.1.call-start = ((), (), s32[]{:S(2)}) async-start(), calls=%async_computation.4 | async-start | bytes 786432 | tf_op jit(solution)/shard_map/psum | solution.py:254
Sparse Core Ops, SparseCore 0:
  9.5 31.9 all-gather.4
  119.7 60.6 reduce-scatter.3
  214.1 52.0 all-reduce.2
where the time goes:
time: 276 us; the launch traced here: 275 us
  waiting for transfers between devices  126 us (46%)
  blocking collectives  60.4 us (22%)
  matrix products  29.3 us (11%)
  local copies, waits for them, and re-layouts  20 us (7%)
  between operations  17.2 us (6%)
  other arithmetic  10.9 us (4%)
  starting transfers between devices  10.7 us (4%)
    unnamed x4, waiting for transfers between devices  61.5 us
    psum x1, waiting for transfers between devices, shards(): lax.psum(term.astype(jnp.bfloat16), ('seq', 'dp')).astype(jnp.float32)  51.6 us
    psum x1, blocking collectives, shards(): lax.psum(judge_part.astype(jnp.bfloat16), 'segment').astype(jnp.float32)  19.9 us
    psum x1, blocking collectives, from_root(): return lax.psum(kept, axis)  15.5 us
    all_gather x2, blocking collectives, forward(): latent_all = lax.all_gather(latent_local, 'seq', axis=0, tiled=True)  11.7 us
    another operation x14, local copies, waits for them, and re-layouts  10.8 us
    dot_general x1, matrix products, condition(): return jnp.dot(hidden, mod_w, preferred_element_type=jnp.float32)  10.6 us
    all_to_all x2, waiting for transfers between devices, forward(): lax.all_to_all(head_out, 'seq', split_axis=0, concat_axis=1, tiled=True)  8.52 us
  transfers between devices with their start and end apart: 6, of which 5 were waited for; matrix products, arithmetic and copies ran while one was open for 9% of the time, Pallas kernels for 0%

commit v1 on v0

--- a/solution.py
+++ b/solution.py
@@ -7,6 +7,12 @@
 SHIFT = 7.0
 EPS = 1e-06
 ADV_WEIGHT = 3.0
+
+
+def summed_here(x, name):
+    shards = lax.all_gather(x, name, axis=0, tiled=False)
+    result = shards.sum(axis=0)
+    return result
 
 
 def from_root(value, axis, source):
@@ -232,7 +238,7 @@
     real_term, fake_term, adverse_term = (
         lax.psum(real_part.astype(jnp.bfloat16), "segment").astype(jnp.float32),
         lax.psum(fake_part.astype(jnp.bfloat16), "segment").astype(jnp.float32),
-        lax.psum(judge_part.astype(jnp.bfloat16), "segment").astype(jnp.float32),
+        summed_here(judge_part.astype(jnp.bfloat16), "segment").astype(jnp.float32),
     )
     error_local = jnp.sum(jnp.abs(sample - noisy_critic.astype(jnp.float32) + real_term))
     error_total = lax.psum(error_local, "seq")

time: 276 us -> 267 us (0.967)
  waiting for transfers between devices: 126 us -> 65.8 us
  blocking collectives: 60.4 us -> 113 us
    unnamed x4, waiting for transfers between devices: 61.5 us -> 0.73 us
    psum x1, blocking collectives: 19.9 us -> 60.4 us  [shards(): lax.psum(real_part.astype(jnp.bfloat16), 'segment').astype(jnp.float32)]
    all_gather x0 -> x1, blocking collectives: none -> 12 us  [summed_here(): shards = lax.all_gather(x, name, axis=0, tiled=False)]
  transfers between devices with their start and end apart: 6 -> 6, of which waited for: 5 -> 4; matrix products, arithmetic and copies ran while one was open for 9% -> 10% of each run, Pallas kernels for 0% -> 0%
where the time goes in v1:
time: 267 us; the launch traced here: 265 us
  blocking collectives  113 us (42%)
  waiting for transfers between devices  65.8 us (25%)
  matrix products  29.3 us (11%)
  local copies, waits for them, and re-layouts  18.5 us (7%)
  between operations  17.2 us (6%)
  other arithmetic  11 us (4%)
  starting transfers between devices  10.7 us (4%)
    psum x1, blocking collectives, shards(): lax.psum(real_part.astype(jnp.bfloat16), 'segment').astype(jnp.float32)  60.4 us
    psum x1, waiting for transfers between devices, shards(): lax.psum(term.astype(jnp.bfloat16), ('seq', 'dp')).astype(jnp.float32)  52 us
    psum x1, blocking collectives, from_root(): return lax.psum(kept, axis)  15.5 us
    all_gather x1, blocking collectives, summed_here(): shards = lax.all_gather(x, name, axis=0, tiled=False)  12 us
    all_gather x2, blocking collectives, forward(): latent_all = lax.all_gather(latent_local, 'seq', axis=0, tiled=True)  11.7 us
    dot_general x1, matrix products, condition(): return jnp.dot(hidden, mod_w, preferred_element_type=jnp.float32)  10.6 us
    another operation x14, local copies, waits for them, and re-layouts  10.2 us
    all_to_all x2, waiting for transfers between devices, forward(): lax.all_to_all(head_out, 'seq', split_axis=0, concat_axis=1, tiled=True)  8.52 us
  transfers between devices with their start and end apart: 6, of which 4 were waited for; matrix products, arithmetic and copies ran while one was open for 10% of the time, Pallas kernels for 0%

profile of v1, /device:TPU:0, one launch (start us, length us, event | category | flops | bytes accessed | tf_op | source)
XLA Modules:
  0.0 265.5 jit_solution(8640600513980821520)
XLA Ops:
  7.2 0.7 all-gather.6.cloned.1.call-update
  7.9 0.7 constant_dynamic-slice_fusion
  8.6 0.6 fusion.98
  11.1 1.0 fusion.37
  12.2 0.9 fusion.97
  13.2 10.6 %fusion.34 = f32[1,1,3840]{2,1,0:T(1,128)S(1)} fusion(bf16[3072,1]{0,1:T(2,128)(2,1)S(1)} %reshape.224, bf16[1,3072,3840]{2,1,0:T(8,128)(2,1)} %param.31), kind=kOutput, calls=%fused_computation.97 | convolution fusion | flops 23592960 | bytes 23614464 | tf_op jit(solution)/shard_map/dot_general | solution.py:40
  23.8 6.7 %all-gather.3 = f32[4,1,3840]{2,1,0:T(1,128)S(1)} all-gather(f32[1,1,3840]{2,1,0:T(1,128)S(1)} %fusion.34), channel_id=1, replica_groups=mesh['segment'=4,'seq'=4,'dp'=2] {'seq'}, dimensions={0}, use_global_device_ids=true | all-gather | bytes 76800 | tf_op jit(solution)/shard_map/all_gather | solution.py:139
  30.4 6.0 %all-gather = bf16[1,512,64]{1,2,0:T(8,128)(2,1)S(1)} all-gather(bf16[1,128,64]{1,2,0:T(8,128)(2,1)S(1)} %add_convert_fusion.6), channel_id=2, replica_groups=mesh['segment'=4,'seq'=4,'dp'=2] {'seq'}, dimensions={1}, use_global_device_ids=true | all-gather | bytes 81920 | tf_op jit(solution)/shard_map/all_gather | solution.py:155
  36.4 0.6 fusion.96
  37.1 9.9 %conditional.7 = (bf16[512,128]{1,0:T(8,128)(2,1)}) conditional(s32[]{:T(128)} %convert_element_type.189, () %tuple.57, (bf16[512,64]{0,1:T(8,128)(2,1)S(1)}, bf16[64,3072]{1,0:T(8,128)(2,1)S(1)}, f32[3072]{0:T(1024)}, f32[3072]{0:T(1024)}, bf16[1,3072,1,3,128]{4,1,3,2,0:T(8,128)(2,1)S(1)}, /*index=5*/f32[2,128]{1,0:T(2,128)S(1)}) %tuple.157), branch_computations={%region_0.1_spmd, %region_1.7_spmd} | conditional | flops 1559433216 | bytes 40133668 | solution.py:104
  37.1 0.7 broadcast_add_fusion
  37.8 2.4 copy.53
  40.2 1.1 fusion.91
  41.3 0.8 multiply_reduce_fusion
  42.1 0.9 copy-done.13
  43.0 2.4 fusion
  45.5 0.4 fusion.92
  46.0 1.0 convolution_convert_fusion
  47.0 3.3 %all-to-all-start = ((bf16[4,128,128]{2,1,0:T(8,128)(2,1)}), bf16[4,128,128]{2,1,0:T(8,128)(2,1)S(1)}, u32[]{:S(2)}, u32[]{:S(2)}) async-start(bf16[4,128,128]{2,1,0:T(8,128)(2,1)} %bitcast.26), calls=%async_computation | async-start | bytes 262144 | tf_op jit(solution)/shard_map/all_to_all | solution.py:164
  51.0 3.9 %all-to-all-done = bf16[4,128,128]{2,1,0:T(8,128)(2,1)S(1)} async-done(((bf16[4,128,128]{2,1,0:T(8,128)(2,1)}), bf16[4,128,128]{2,1,0:T(8,128)(2,1)S(1)}, u32[]{:S(2)}, u32[]{:S(2)}) %all-to-all-start) | async-done | bytes 131104 | tf_op jit(solution)/shard_map/all_to_all | solution.py:164
  54.9 3.4 %conditional.8 = (f32[128,3072]{1,0:T(8,128)S(1)}) conditional(s32[]{:T(128)} %convert_element_type.189, () %tuple.56, (bf16[128,4,128]{2,0,1:T(8,128)(2,1)S(1)}, bf16[4,128,3072]{2,1,0:T(8,128)(2,1)}) %tuple.152), branch_computations={%region_7.8_spmd, %region_8.10_spmd} | conditional | flops 406978560 | bytes 11141128 | solution.py:104
  54.9 2.9 %convolution_convert_fusion.1 = bf16[4,128,3072]{2,1,0:T(8,128)(2,1)S(1)} fusion(bf16[128,4,128]{2,0,1:T(8,128)(2,1)S(1)} %get-tuple-element.132, bf16[4,128,3072]{2,1,0:T(8,128)(2,1)} %get-tuple-element.133), kind=kOutput, calls=%fused_computation.28 | convolution fusion | flops 404226048 | bytes 6422528 | tf_op jit(solution)/shard_map/cond/branch_1_fun/thk,hkd->htd/dot_general | solution.py:168
  57.7 0.6 convert_reduce_fusion
  58.3 0.5 fusion.99
  59.5 0.9 copy-done.7
  60.4 0.4 fusion.44
  60.8 15.5 %psum.35 = bf16[128,64]{0,1:T(8,128)(2,1)S(1)} all-reduce(bf16[128,64]{0,1:T(8,128)(2,1)S(1)} %fusion.44), channel_id=1, replica_groups=mesh['segment'=4,'seq'=4,'dp'=2] {'segment'}, use_global_device_ids=true, to_apply=%region_12.13 | all-reduce | flops 8192 | bytes 32768 | tf_op jit(solution)/shard_map/psum | solution.py:20
  76.4 5.7 %all_gather.21 = bf16[512,64]{0,1:T(8,128)(2,1)} all-gather(bf16[128,64]{0,1:T(8,128)(2,1)S(1)} %fusion.56), channel_id=1, replica_groups=mesh['segment'=4,'seq'=4,'dp'=2] {'seq'}, dimensions={0}, use_global_device_ids=true | all-gather | bytes 81920 | tf_op jit(solution)/shard_map/all_gather | solution.py:155
  82.1 5.8 %conditional.9 = (bf16[512,128]{1,0:T(8,128)(2,1)S(1)}, f32[512,128]{0,1:T(8,128)}, f32[512,1]{0,1:T(1,128)}, f32[512,128]{0,1:T(8,128)}, f32[512,1]{0,1:T(1,128...) conditional(s32[]{:T(128)} %convert_element_type.196, () %tuple.61, ...), branch_computations={%region_13.14_spmd, %region_14.20_spmd} | conditional | flops 1559433216 | bytes 43594936 | solution.py:104
  82.1 0.6 broadcast.304.clone
  82.7 0.6 broadcast.304
  83.3 0.7 broadcast.302.clone2.1
  83.9 0.7 broadcast.302.clone2
  84.6 0.7 broadcast.302.clone
  85.3 0.7 broadcast.303.clone
  86.0 0.8 broadcast.303
  86.8 1.1 broadcast.305
  87.9 0.7 copy-done.15
  88.5 3.9 %all-to-all-start.1 = ((bf16[4,128,128]{2,1,0:T(8,128)(2,1)}), bf16[4,128,128]{2,1,0:T(8,128)(2,1)}, u32[]{:S(2)}, u32[]{:S(2)}) async-start(bf16[4,128,128]{2,1,0:T(8,128)(2,1)} %bitcast.136), calls=%async_computation.1 | async-start | bytes 262144 | tf_op jit(solution)/shard_map/all_to_all | solution.py:164
  92.5 4.7 %all-to-all-done.1 = bf16[4,128,128]{2,1,0:T(8,128)(2,1)} async-done(((bf16[4,128,128]{2,1,0:T(8,128)(2,1)}), bf16[4,128,128]{2,1,0:T(8,128)(2,1)}, u32[]{:S(2)}, u32[]{:S(2)}) %all-to-all-start.1) | async-done | bytes 131104 | tf_op jit(solution)/shard_map/all_to_all | solution.py:164
  97.2 1.3 conditional.10
  97.2 1.3 broadcast.311
  98.5 1.9 fusion.100
  100.8 1.2 add_convert_fusion.4
  102.0 2.1 select_convert_fusion
  104.1 0.7 fusion.90
  104.8 2.0 multiply_convert_fusion.9
  106.8 0.7 conditional.11
  106.8 0.7 broadcast.312
  107.5 3.3 %all-to-all-start.2 = ((bf16[128,4,128]{0,2,1:T(8,128)(2,1)}), bf16[128,4,128]{0,2,1:T(8,128)(2,1)S(1)}, u32[]{:S(2)}, u32[]{:S(2)}) async-start(bf16[128,4,128]{0,2,1:T(8,128)(2,1)} %bitcast.33), calls=%async_computation.2 | async-start | bytes 262144 | tf_op jit(solution)/shard_map/all_to_all | solution.py:210
  110.9 4.5 %all-to-all-done.2 = bf16[128,4,128]{0,2,1:T(8,128)(2,1)S(1)} async-done(((bf16[128,4,128]{0,2,1:T(8,128)(2,1)}), bf16[128,4,128]{0,2,1:T(8,128)(2,1)S(1)}, u32[]{:S(2)}, u32[]{:S(2)}) %all-to-all-start.2) | async-done | bytes 131104 | tf_op jit(solution)/shard_map/all_to_all | solution.py:210
  115.4 0.7 copy-done.11
  116.2 1.0 copy-done.4
  117.4 0.7 copy.71
  118.3 60.4 %all-reduce = (bf16[128,64]{0,1:T(8,128)(2,1)S(1)}, bf16[128,64]{0,1:T(8,128)(2,1)S(1)}) all-reduce(bf16[128,64]{0,1:T(8,128)(2,1)} %get-tuple-element.342, bf16[128,64]{0,1:T(8,128)(2,1)} %get-tuple-element.341), channel_id=1, replica_groups=mesh['segment'=4,'seq'=4,'dp'=2] {'segment'}, use_global_device_ids=true, to_apply=%region_25.26 | all-reduce | flops 16384 | bytes 65536 | tf_op jit(solution)/shard_map/psum | solution.py:239
  178.6 1.3 fusion.54
  180.0 6.5 %psum.38 = f32[]{:T(128)} all-reduce(f32[]{:T(128)} %fusion.54), channel_id=1, replica_groups=mesh['segment'=4,'seq'=4,'dp'=2] {'seq'}, use_global_device_ids=true, to_apply=%region_28.29 | all-reduce | flops 1 | bytes 8 | tf_op jit(solution)/shard_map/psum | solution.py:244
  187.0 0.8 copy.72
  187.9 2.5 fusion.43
  190.3 12.0 %all-gather.2 = bf16[512,64]{0,1:T(8,128)(2,1)S(1)} all-gather(bf16[128,64]{0,1:T(8,128)(2,1)S(1)} %fusion.43), channel_id=4, replica_groups=mesh['segment'=4,'seq'=4,'dp'=2] {'segment'}, dimensions={0}, use_global_device_ids=true | all-gather | bytes 81920 | tf_op jit(solution)/shard_map/all_gather | solution.py:13
  202.5 1.9 convolution_convert_fusion.6
  204.4 0.6 fusion.89
  205.0 52.0 %all-reduce.3.cloned.1.call-done = bf16[3072,64]{0,1:T(8,128)(2,1)} async-done(((bf16[3072,64]{0,1:T(8,128)(2,1)}), bf16[3072,64]{0,1:T(8,128)(2,1)}) %all-reduce.3.cloned.1.call-update) | async-done | bytes 393232 | tf_op jit(solution)/shard_map/psum | solution.py:260
  257.0 1.9 multiply_bitcast_fusion
  (78 shorter events, 2.1 us)
Async XLA Ops:
  7.2 3.9 %copy-start = (bf16[1,256,3072]{2,1,0:T(8,128)(2,1)S(1)}, bf16[1,256,3072]{2,1,0:T(8,128)(2,1)}, u32[]{:S(2)}) copy-start(bf16[1,256,3072]{2,1,0:T(8,128)(2,1)} %param.30) | copy-start | bytes 4718596
  7.2 47.7 %all-gather.6.cloned.1.call-start = ((), (), s32[]{:S(2)}) async-start(), calls=%async_computation.5 | async-start | bytes 3932160 | tf_op jit(solution)/shard_map/all_gather | solution.py:143
  13.2 17.3 %copy-start.26 = (bf16[1,128,64]{1,2,0:T(8,128)(2,1)S(1)}, bf16[1,128,64]{1,2,0:T(8,128)(2,1)}, u32[]{:S(2)}) copy-start(bf16[1,128,64]{1,2,0:T(8,128)(2,1)} %param.25) | copy-start | bytes 49156
  13.2 23.9 %copy-start.3 = (bf16[1,3072,1,3,128]{4,1,3,2,0:T(8,128)(2,1)S(1)}, bf16[1,3072,1,3,128]{4,1,3,2,0:T(8,128)(2,1)}, u32[]{:S(2)}) copy-start(bf16[1,3072,1,3,128]{4,1,3,2,0:T(8,128)(2,1)} %param.32) | copy-start | bytes 7077892
  13.2 23.9 %copy-start.5 = (bf16[1,64,3072]{2,1,0:T(8,128)(2,1)S(1)}, bf16[1,64,3072]{2,1,0:T(8,128)(2,1)}, u32[]{:S(2)}) copy-start(bf16[1,64,3072]{2,1,0:T(8,128)(2,1)} %param.29) | copy-start | bytes 1179652
  13.2 23.9 %copy-start.28 = (f32[1,2,128]{2,1,0:T(2,128)S(1)}, f32[1,2,128]{2,1,0:T(2,128)}, u32[]{:S(2)}) copy-start(f32[1,2,128]{2,1,0:T(2,128)} %param.34) | copy-start | bytes 3076
  37.0 21.3 %copy-start.18 = (f32[3072]{0:T(1024)}, f32[3072]{0:T(1024)S(1)}, u32[]{:S(2)}) copy-start(f32[3072]{0:T(1024)S(1)} %get-tuple-element.340) | copy-start | bytes 36868
  37.0 22.1 %copy-start.20 = (f32[3072]{0:T(1024)}, f32[3072]{0:T(1024)S(1)}, u32[]{:S(2)}) copy-start(f32[3072]{0:T(1024)S(1)} %get-tuple-element.337) | copy-start | bytes 36868
  37.0 22.1 %copy-start.24 = (f32[3072]{0:T(1024)}, f32[3072]{0:T(1024)S(1)}, u32[]{:S(2)}) copy-start(f32[3072]{0:T(1024)S(1)} %get-tuple-element.336) | copy-start | bytes 36868
  41.3 1.7 copy-start.13
  47.0 7.9 %all-to-all-start = ((bf16[4,128,128]{2,1,0:T(8,128)(2,1)}), bf16[4,128,128]{2,1,0:T(8,128)(2,1)S(1)}, u32[]{:S(2)}, u32[]{:S(2)}) async-start(bf16[4,128,128]{2,1,0:T(8,128)(2,1)} %bitcast.26), calls=%async_computation | async-start | bytes 262144 | tf_op jit(solution)/shard_map/all_to_all | solution.py:164
  51.0 25.4 %copy-start.23 = (bf16[1,128,64]{1,2,0:T(8,128)(2,1)}, bf16[1,128,64]{1,2,0:T(8,128)(2,1)S(1)}, u32[]{:S(2)}) copy-start(bf16[1,128,64]{1,2,0:T(8,128)(2,1)S(1)} %copy.74) | copy-start | bytes 49156
  58.3 2.1 copy-start.9
  59.5 0.9 copy-start.7
  76.4 5.7 %copy-start.17 = (bf16[128,64]{0,1:T(8,128)(2,1)}, bf16[128,64]{0,1:T(8,128)(2,1)S(1)}, u32[]{:S(2)}) copy-start(bf16[128,64]{0,1:T(8,128)(2,1)S(1)} %psum.35) | copy-start | bytes 49156
  82.1 15.0 %copy-start.2 = (bf16[4,1,128,3072]{3,2,1,0:T(8,128)(2,1)S(1)}, bf16[4,1,128,3072]{3,2,1,0:T(8,128)(2,1)}, u32[]{:S(2)}) copy-start(bf16[4,1,128,3072]{3,2,1,0:T(8,128)(2,1)} %all-gather.6.cloned.1.call-done) | copy-start | bytes 9437188
  87.9 0.7 copy-start.15
  88.5 8.6 %all-to-all-start.1 = ((bf16[4,128,128]{2,1,0:T(8,128)(2,1)}), bf16[4,128,128]{2,1,0:T(8,128)(2,1)}, u32[]{:S(2)}, u32[]{:S(2)}) async-start(bf16[4,128,128]{2,1,0:T(8,128)(2,1)} %bitcast.136), calls=%async_computation.1 | async-start | bytes 262144 | tf_op jit(solution)/shard_map/all_to_all | solution.py:164
  98.5 2.3 copy-start.21
  98.5 2.3 copy-start.25
  98.5 3.5 %copy-start.10 = (bf16[1,3072,64]{1,2,0:T(8,128)(2,1)S(1)}, bf16[1,3072,64]{1,2,0:T(8,128)(2,1)}, u32[]{:S(2)}) copy-start(bf16[1,3072,64]{1,2,0:T(8,128)(2,1)} %param.35) | copy-start | bytes 1179652
  100.8 4.0 %copy-start.19 = (f32[3072]{0:T(1024)S(1)}, f32[3072]{0:T(1024)}, u32[]{:S(2)}) copy-start(f32[3072]{0:T(1024)} %copy-done.18) | copy-start | bytes 36868
  104.1 0.7 copy-start.16
  107.5 7.9 %all-to-all-start.2 = ((bf16[128,4,128]{0,2,1:T(8,128)(2,1)}), bf16[128,4,128]{0,2,1:T(8,128)(2,1)S(1)}, u32[]{:S(2)}, u32[]{:S(2)}) async-start(bf16[128,4,128]{0,2,1:T(8,128)(2,1)} %bitcast.33), calls=%async_computation.2 | async-start | bytes 262144 | tf_op jit(solution)/shard_map/all_to_all | solution.py:210
  110.8 76.2 %reduce-scatter.4.cloned.1.call-start = ((), (), s32[]{:S(2)}) async-start(), calls=%async_computation.6 | async-start | bytes 163840
  115.4 1.8 copy-start.4
  115.4 0.7 copy-start.11
  117.2 85.3 %copy-start.8 = (bf16[128,3072]{1,0:T(8,128)(2,1)S(1)}, bf16[128,3072]{1,0:T(8,128)(2,1)}, u32[]{:S(2)}) copy-start(bf16[128,3072]{1,0:T(8,128)(2,1)} %copy-done.7) | copy-start | bytes 2359300
  118.2 140.8 %copy-start.1 = (bf16[1,256,3072]{2,1,0:T(8,128)(2,1)S(1)}, bf16[1,256,3072]{2,1,0:T(8,128)(2,1)}, u32[]{:S(2)}) copy-start(bf16[1,256,3072]{2,1,0:T(8,128)(2,1)} %param.30) | copy-start | bytes 4718596
  118.2 138.8 %all-reduce.3.cloned.1.call-start = ((), (), s32[]{:S(2)}) async-start(), calls=%async_computation.4 | async-start | bytes 786432 | tf_op jit(solution)/shard_map/psum | solution.py:260
Sparse Core Ops, SparseCore 0:
  9.5 31.9 all-gather.5
  118.3 60.4 reduce-scatter.3
  204.5 52.5 all-reduce.2
